TPU v7x, 32 devices: a whole 2x2x4 slice. The times are simulated.
32 devices in a mesh: expert: 16 (over z, x, core), tensor: 2 (over y).
Axes of the slice: x: 2, y: 2, z: 4, core: 2. Of those that a mesh axis runs over, the one named last changes fastest.
Arguments:
- tokens: bfloat16 [2048, 2048], P('expert', 'tensor'), may hold values from -6 to 6
- cotangent: bfloat16 [2048, 2048], P('expert', 'tensor'), may hold values from -6 to 6
- route_ids: int32 [2048, 6], P('expert'), may hold values from 0 to 15, all different within a row
- route_weights: float32 [2048, 6], P('expert'), may hold values from 0.05 to 0.5
- shared_gate: bfloat16 [1408, 2048], P('tensor'), may hold values from -0.125 to 0.125
- shared_up: bfloat16 [1408, 2048], P('tensor'), may hold values from -0.125 to 0.125
- shared_down: bfloat16 [1408, 2048], P('tensor'), may hold values from -0.15625 to 0.15625
- expert_gate: bfloat16 [16, 1408, 2048], P('expert', 'tensor'), may hold values from -0.125 to 0.125
- expert_up: bfloat16 [16, 1408, 2048], P('expert', 'tensor'), may hold values from -0.125 to 0.125
- expert_down: bfloat16 [16, 1408, 2048], P('expert', 'tensor'), may hold values from -0.15625 to 0.15625
Outputs:
- layer_output: bfloat16 [2048, 2048], P('expert', 'tensor')
- input_grad: bfloat16 [2048, 2048], P('expert', 'tensor')
Inputs may be any that keep to these rules, and one draw needn't show every extreme that they name: `route_ids`: each row names 6 different experts.
All inputs are finite; a program needn't handle non-finite values.
Results may differ from a plain program's by a relative error of at most 0.0051.
Values may be sent and summed in bfloat16 or wider, within the bound.
No kernel may reach another device: no remote copies, remote signals or barrier semaphores. Data moves between devices by JAX's collectives and lax.ppermute only.
A program may use at most 64 MiB of HBM per device.

v0:
```python
import jax
import jax.numpy as jnp
from jax import lax
from jax.sharding import PartitionSpec as P


def silu_parts(pre_act):
    sigmoid_value = jax.nn.sigmoid(pre_act)
    return (pre_act * sigmoid_value, sigmoid_value * (1.0 + pre_act * (1.0 - sigmoid_value)))


def on_device(
    tokens,
    cotangent,
    route_ids,
    route_weights,
    shared_gate,
    shared_up,
    shared_down,
    expert_gate,
    expert_up,
    expert_down,
):
    expert_count = lax.axis_size("expert")
    tok_rows, top_count = route_ids.shape
    local_experts = expert_gate.shape[0]
    all_experts = local_experts * expert_count
    capacity = tok_rows * top_count // (2 * all_experts)
    slot_total = all_experts * capacity
    flat_ids = route_ids.reshape(-1)
    one_hot = (flat_ids[:, None] == jnp.arange(all_experts, dtype=jnp.int32)[None, :]).astype(
        jnp.int32
    )
    rank_in = jnp.sum((jnp.cumsum(one_hot, axis=0) - one_hot) * one_hot, axis=1)
    kept_mask = rank_in < capacity
    slot_index = jnp.where(kept_mask, flat_ids * capacity + rank_in, slot_total)
    slot_match = jnp.arange(slot_total, dtype=jnp.int32)[:, None] == slot_index[None, :]
    dispatch = jnp.any(slot_match.reshape(slot_total, tok_rows, top_count), axis=2).astype(
        jnp.bfloat16
    )
    gate_flat = route_weights.reshape(-1)
    slot_gate = jnp.sum(jnp.where(slot_match, gate_flat[None, :], 0.0), axis=1)
    gate_dispatch = dispatch.astype(jnp.float32) * slot_gate[:, None]
    x_full, c_full = (
        lax.all_gather(tokens, "tensor", axis=1, tiled=True),
        lax.all_gather(cotangent, "tensor", axis=1, tiled=True),
    )
    x_slots = jnp.dot(dispatch, tokens, preferred_element_type=jnp.float32).astype(jnp.bfloat16)
    g_slots = (
        slot_gate[:, None] * jnp.dot(dispatch, cotangent, preferred_element_type=jnp.float32)
    ).astype(jnp.bfloat16)
    x_part, g_part = (
        lax.all_to_all(x_slots, "expert", split_axis=0, concat_axis=0, tiled=True),
        lax.all_to_all(g_slots, "expert", split_axis=0, concat_axis=0, tiled=True),
    )
    x_recv, g_recv = (
        lax.all_gather(x_part, "tensor", axis=1, tiled=True),
        lax.all_gather(g_part, "tensor", axis=1, tiled=True),
    )

    def owner_layout(values):
        shaped = values.reshape(expert_count, local_experts, capacity, values.shape[-1])
        return shaped.transpose(1, 0, 2, 3).reshape(
            local_experts, expert_count * capacity, values.shape[-1]
        )

    def source_layout(values):
        shaped = values.reshape(local_experts, expert_count, capacity, values.shape[-1])
        return shaped.transpose(1, 0, 2, 3).reshape(slot_total, values.shape[-1])

    x_own = owner_layout(x_recv)
    g_own = owner_layout(g_recv)
    gate_pre = jnp.einsum("erd,efd->erf", x_own, expert_gate, preferred_element_type=jnp.float32)
    up_pre = jnp.einsum("erd,efd->erf", x_own, expert_up, preferred_element_type=jnp.float32)
    act_value, act_slope = silu_parts(gate_pre)
    hidden = (act_value * up_pre).astype(jnp.bfloat16)
    grad_hidden = jnp.einsum("erd,efd->erf", g_own, expert_down, preferred_element_type=jnp.float32)
    grad_gate = (grad_hidden * up_pre * act_slope).astype(jnp.bfloat16)
    grad_up = (grad_hidden * act_value).astype(jnp.bfloat16)
    value_part = source_layout(
        jnp.einsum("erf,efd->erd", hidden, expert_down, preferred_element_type=jnp.float32).astype(
            jnp.bfloat16
        )
    )
    grads_joined = jnp.concatenate((grad_gate, grad_up), axis=2)
    weights_joined = jnp.concatenate((expert_gate, expert_up), axis=1)
    input_term = jnp.einsum(
        "erf,efd->erd", grads_joined, weights_joined, preferred_element_type=jnp.float32
    )
    input_part = source_layout(input_term.astype(jnp.bfloat16))
    shared_gate_pre = jnp.einsum(
        "td,fd->tf", x_full, shared_gate, preferred_element_type=jnp.float32
    )
    shared_up_pre = jnp.einsum("td,fd->tf", x_full, shared_up, preferred_element_type=jnp.float32)
    shared_act, shared_slope = silu_parts(shared_gate_pre)
    shared_hidden = (shared_act * shared_up_pre).astype(jnp.bfloat16)
    shared_value = jnp.dot(shared_hidden, shared_down, preferred_element_type=jnp.float32)
    shared_grad_hidden = jnp.einsum(
        "td,fd->tf", c_full, shared_down, preferred_element_type=jnp.float32
    )
    shared_grad_gate = (shared_grad_hidden * shared_up_pre * shared_slope).astype(jnp.bfloat16)
    shared_grad_up = (shared_grad_hidden * shared_act).astype(jnp.bfloat16)
    shared_input = jnp.dot(shared_grad_gate, shared_gate, preferred_element_type=jnp.float32)
    shared_input = shared_input + jnp.dot(
        shared_grad_up, shared_up, preferred_element_type=jnp.float32
    )
    value_back, input_back = (
        lax.all_to_all(value_part, "expert", split_axis=0, concat_axis=0, tiled=True),
        lax.all_to_all(input_part, "expert", split_axis=0, concat_axis=0, tiled=True),
    )
    early_value = shared_value + jnp.einsum(
        "st,sd->td",
        gate_dispatch,
        value_back.astype(jnp.float32),
        precision=lax.Precision.HIGHEST,
        preferred_element_type=jnp.float32,
    )
    early_input = shared_input + jnp.einsum(
        "st,sd->td",
        dispatch,
        input_back,
        precision=lax.Precision.HIGHEST,
        preferred_element_type=jnp.float32,
    )
    value_total, input_total = (
        lax.psum_scatter(early_value, "tensor", scatter_dimension=1, tiled=True),
        lax.psum_scatter(early_input, "tensor", scatter_dimension=1, tiled=True),
    )
    return (value_total.astype(jnp.bfloat16), input_total.astype(jnp.bfloat16))


def solution(mesh):
    in_specs = (
        P("expert", "tensor"),
        P("expert", "tensor"),
        P("expert", None),
        P("expert", None),
        P("tensor", None),
        P("tensor", None),
        P("tensor", None),
        P("expert", "tensor", None),
        P("expert", "tensor", None),
        P("expert", "tensor", None),
    )
    out_specs = (P("expert", "tensor"), P("expert", "tensor"))
    return jax.shard_map(
        on_device, mesh=mesh, in_specs=in_specs, out_specs=out_specs, check_vma=False
    )
```

profile of v0, /device:TPU:0, one launch (start us, length us, event | category | flops | bytes accessed | tf_op | source)
XLA Modules:
  0.0 222.2 jit_solution(5177407489219410796)
XLA Ops:
  7.2 0.0 copy-start
  7.2 0.9 copy.19
  8.1 0.1 eq.50
  8.3 0.1 eq.46
  8.4 0.7 broadcast_multiply_fusion
  9.1 1.7 reduce-window.6
  10.8 0.3 slice_reduce_fusion
  11.1 0.1 fusion.35
  11.2 0.0 copy-start.11
  11.2 0.1 reduce_sum.21
  11.4 0.1 copy.23
  11.5 0.1 copy.24
  11.5 0.2 fusion.16
  11.7 0.0 copy-start.8
  11.7 2.3 %convolution_convert_fusion = bf16[384,1024]{1,0:T(8,128)(2,1)} fusion(pred[384,128]{1,0:T(8,128)(4,1)S(1)} %fusion.16, bf16[128,1024]{1,0:T(8,128)(2,1)} %param.10), kind=kOutput, calls=%fused_computation.18 | convolution fusion | flops 101056512 | bytes 1097728 | tf_op jit(solution)/shard_map/dot_general | solution.py:48
  14.0 7.4 %all-to-all-start = ((bf16[16,24,1024]{2,1,0:T(8,128)(2,1)}), bf16[16,24,1024]{2,1,0:T(8,128)(2,1)}, u32[]{:S(2)}, u32[]{:S(2)}) async-start(bf16[16,24,1024]{2,1,0:T(8,128)(2,1)} %bitcast.74), calls=%async_computation | async-start | bytes 1572864 | tf_op jit(solution)/shard_map/all_to_all | solution.py:53
  21.4 0.0 all-gather.3.cloned.1.call-start
  21.5 0.1 copy.25
  21.6 0.1 broadcast_in_dim.27
  21.7 0.2 select_reduce_fusion
  21.9 18.2 %all-to-all-done = bf16[16,24,1024]{2,1,0:T(8,128)(2,1)} async-done(((bf16[16,24,1024]{2,1,0:T(8,128)(2,1)}), bf16[16,24,1024]{2,1,0:T(8,128)(2,1)}, u32[]{:S(2)}, u32[]{:S(2)}) %all-to-all-start) | async-done | bytes 786464 | tf_op jit(solution)/shard_map/all_to_all | solution.py:53
  40.1 0.0 all-gather.3.cloned.1.call-update
  40.2 0.0 all-gather.5.cloned.1.call-start
  40.2 0.0 copy-done.8
  40.2 0.4 multiply_convert_fusion
  40.6 25.4 %all_to_all.48 = bf16[16,24,1024]{2,1,0:T(8,128)(2,1)} all-to-all(bf16[16,24,1024]{2,1,0:T(8,128)(2,1)S(1)} %bitcast.76), channel_id=1, replica_groups=mesh['expert'=16,'tensor'=2] {'expert'}, dimensions={0} | all-to-all | bytes 1572864 | tf_op jit(solution)/shard_map/all_to_all | solution.py:54
  66.0 0.0 copy-done.9
  66.0 0.0 all-gather.5.cloned.1.call-update
  66.0 2.2 %all-gather.3.cloned.1.call-done = bf16[384,2048]{1,0:T(8,128)(2,1)} async-done(((bf16[384,1024]{1,0:T(8,128)(2,1)}), bf16[384,2048]{1,0:T(8,128)(2,1)}) %all-gather.3.cloned.1.call-update) | async-done | bytes 1572880 | tf_op jit(solution)/shard_map/all_gather | solution.py:57
  68.3 5.1 %fusion.7 = f32[384,704]{0,1:T(8,128)} fusion(bf16[384,2048]{1,0:T(8,128)(2,1)} %all-gather.3.cloned.1.call-done, bf16[1,704,2048]{2,1,0:T(8,128)(2,1)} %param.18), kind=kOutput, calls=%fused_computation.8 | convolution fusion | flops 1107296256 | bytes 5537792 | tf_op jit(solution)/shard_map/erd,efd->erf/dot_general | solution.py:74
  73.4 0.0 copy-done.13
  73.4 2.7 %fusion.9 = f32[384,704]{0,1:T(8,128)} fusion(bf16[384,2048]{1,0:T(8,128)(2,1)S(1)} %copy-done.15, bf16[1,704,2048]{2,1,0:T(8,128)(2,1)S(1)} %copy-done.13), kind=kOutput, calls=%fused_computation.10 | convolution fusion | flops 1107296256 | bytes 5537792 | tf_op jit(solution)/shard_map/erd,efd->erf/dot_general | solution.py:73
  76.0 21.0 %all-gather.5.cloned.1.call-done = bf16[384,2048]{1,0:T(8,128)(2,1)} async-done(((bf16[384,1024]{1,0:T(8,128)(2,1)}), bf16[384,2048]{1,0:T(8,128)(2,1)}) %all-gather.5.cloned.1.call-update) | async-done | bytes 1572880 | tf_op jit(solution)/shard_map/all_gather | solution.py:58
  97.0 4.1 %fusion.21 = (bf16[1,384,704]{1,2,0:T(8,128)(2,1)S(1)}, bf16[1,384,704]{1,2,0:T(8,128)(2,1)S(1)}) fusion(f32[384,704]{0,1:T(8,128)} %fusion.9, f32[384,704]{0,1:T(8,128)} %fusion.7, bf16[384,2048]{1,0:T(8,128)(2,1)} %all-gather.5.cloned.1.call-done, bf16[1,704,2048]{2,1,0:T(8,128)(2,1)S(1)} %copy-done), kind=kOutput, calls=%fused_computation.32 | convolution fusion | flops 1110810624 | bytes 7700480 | tf_op jit(solution)/shard_map/erd,efd->erf/dot_general | solution.py:77
  101.2 3.7 %fusion.14 = bf16[384,2048]{1,0:T(8,128)(2,1)} fusion(bf16[1,704,2048]{2,1,0:T(8,128)(2,1)S(1)} %copy-done.12, bf16[1,704,2048]{2,1,0:T(8,128)(2,1)S(1)} %copy-done.14, bf16[1,384,704]{1,2,0:T(8,128)(2,1)S(1)} %get-tuple-element.3, bf16[1,384,704]{1,2,0:T(8,128)(2,1)S(1)} %get-tuple-element.2), kind=kOutput, calls=%fused_computation.13 | convolution fusion | flops 2229075968 | bytes 8421376 | tf_op jit(solution)/shard_map/erf,efd->erd/dot_general | solution.py:87
  104.9 5.8 %all-to-all-start.3 = ((bf16[16,24,2048]{2,1,0:T(8,128)(2,1)}), bf16[16,24,2048]{2,1,0:T(8,128)(2,1)}, u32[]{:S(2)}, u32[]{:S(2)}) async-start(bf16[16,24,2048]{2,1,0:T(8,128)(2,1)} %bitcast.78), calls=%async_computation.4 | async-start | bytes 3145728 | tf_op jit(solution)/shard_map/all_to_all | solution.py:109
  110.7 0.0 copy-done.7
  110.7 9.2 %all_gather.12 = bf16[128,2048]{1,0:T(8,128)(2,1)S(1)} all-gather(bf16[128,1024]{1,0:T(8,128)(2,1)S(1)} %copy-done.7), channel_id=1, replica_groups=mesh['expert'=16,'tensor'=2] {'tensor'}, dimensions={1}, use_global_device_ids=true | all-gather | bytes 786432 | tf_op jit(solution)/shard_map/all_gather | solution.py:45
  120.0 0.8 copy-done.4
  120.8 2.9 %fusion.44 = f32[128,704]{0,1:T(8,128)S(1)} fusion(bf16[128,2048]{1,0:T(8,128)(2,1)S(1)} %all_gather.12, bf16[704,2048]{1,0:T(8,128)(2,1)} %param.14), kind=kOutput, calls=%fused_computation.62 | convolution fusion | flops 369098752 | bytes 3768320 | tf_op jit(solution)/shard_map/td,fd->tf/dot_general | solution.py:91
  123.7 2.7 %fusion.11 = bf16[384,2048]{1,0:T(8,128)(2,1)} fusion(bf16[1,704,2048]{2,1,0:T(8,128)(2,1)S(1)} %copy-done, f32[384,704]{0,1:T(8,128)S(1)} %copy-done.16, f32[384,704]{0,1:T(8,128)S(1)} %copy-done.17), kind=kOutput, calls=%fused_computation.12 | convolution fusion | flops 1109704704 | bytes 6619136 | tf_op jit(solution)/shard_map/erf,efd->erd/dot_general | solution.py:81
  126.4 16.3 %all-to-all-done.3 = bf16[16,24,2048]{2,1,0:T(8,128)(2,1)} async-done(((bf16[16,24,2048]{2,1,0:T(8,128)(2,1)}), bf16[16,24,2048]{2,1,0:T(8,128)(2,1)}, u32[]{:S(2)}, u32[]{:S(2)}) %all-to-all-start.3) | async-done | bytes 1572896 | tf_op jit(solution)/shard_map/all_to_all | solution.py:109
  142.6 9.2 %all-to-all-start.1 = ((bf16[16,24,2048]{2,1,0:T(8,128)(2,1)}), bf16[16,24,2048]{2,1,0:T(8,128)(2,1)}, u32[]{:S(2)}, u32[]{:S(2)}) async-start(bf16[16,24,2048]{2,1,0:T(8,128)(2,1)} %bitcast.77), calls=%async_computation.1 | async-start | bytes 3145728 | tf_op jit(solution)/shard_map/all_to_all | solution.py:108
  151.8 0.0 reduce-scatter.5.cloned.1.call-start
  151.8 0.0 copy-start.3
  151.9 3.0 %fusion.45 = f32[128,704]{0,1:T(8,128)S(1)} fusion(bf16[128,2048]{1,0:T(8,128)(2,1)} %copy-done.4, bf16[704,2048]{1,0:T(8,128)(2,1)} %param.15), kind=kOutput, calls=%fused_computation.63 | convolution fusion | flops 369098752 | bytes 3768320 | tf_op jit(solution)/shard_map/td,fd->tf/dot_general | solution.py:94
  154.9 9.4 %all_gather.14 = bf16[128,2048]{1,0:T(8,128)(2,1)S(1)} all-gather(bf16[128,1024]{1,0:T(8,128)(2,1)S(1)} %copy-done.8), channel_id=1, replica_groups=mesh['expert'=16,'tensor'=2] {'tensor'}, dimensions={1}, use_global_device_ids=true | all-gather | bytes 786432 | tf_op jit(solution)/shard_map/all_gather | solution.py:46
  164.3 0.9 fusion.46
  165.3 0.9 copy-done.2
  166.2 0.7 fusion.27
  166.9 2.0 fusion.47
  168.9 0.0 copy-done.1
  168.9 0.0 copy-start.10
  168.9 1.6 fusion.15
  170.6 0.0 reduce-scatter.5.cloned.1.call-update
  170.6 0.0 reduce-scatter.3.cloned.1.call-start
  170.6 13.1 %all-to-all-done.1 = bf16[16,24,2048]{2,1,0:T(8,128)(2,1)} async-done(((bf16[16,24,2048]{2,1,0:T(8,128)(2,1)}), bf16[16,24,2048]{2,1,0:T(8,128)(2,1)}, u32[]{:S(2)}, u32[]{:S(2)}) %all-to-all-start.1) | async-done | bytes 1572896 | tf_op jit(solution)/shard_map/all_to_all | solution.py:108
  183.7 2.6 %fusion.23 = f32[128,2048]{1,0:T(8,128)S(1)} fusion(bf16[384,2048]{1,0:T(8,128)(2,1)} %bitcast.7, f32[384]{0:T(512)S(1)} %copy-done.10, pred[384,128]{1,0:T(8,128)(4,1)S(1)} %fusion.16), kind=kOutput, calls=%fused_computation.38 | convolution fusion | flops 1208107008 | bytes 2672128 | tf_op jit(solution)/shard_map/st,sd->td/dot_general | solution.py:111
  186.3 3.4 %convolution_add_fusion.1 = f32[128,2048]{1,0:T(8,128)} fusion(f32[128,2048]{1,0:T(8,128)S(1)} %fusion.23, bf16[704,2048]{1,0:T(8,128)(2,1)} %param.16, f32[128,704]{0,1:T(8,128)S(1)} %copy-done.6, f32[128,704]{0,1:T(8,128)S(1)} %fusion.44), kind=kOutput, calls=%fused_computation.15 | convolution fusion | flops 369901568 | bytes 5701632 | tf_op jit(solution)/shard_map/dot_general | solution.py:97
  189.7 0.0 reduce-scatter.3.cloned.1.call-update
  189.7 1.5 reduce-scatter.5.cloned.1.call-done
  191.2 1.8 convert_element_type.76
  193.0 20.9 %reduce-scatter.3.cloned.1.call-done = f32[128,1024]{1,0:T(8,128)} async-done(((f32[128,2048]{1,0:T(8,128)}), f32[128,1024]{1,0:T(8,128)}) %reduce-scatter.3.cloned.1.call-update) | async-done | bytes 524304 | tf_op jit(solution)/shard_map/reduce_scatter | solution.py:126
  213.9 1.8 convert_element_type.67
  (28 shorter events, 0.1 us)
Async XLA Ops:
  7.2 89.9 %copy-start = (bf16[1,704,2048]{2,1,0:T(8,128)(2,1)S(1)}, bf16[1,704,2048]{2,1,0:T(8,128)(2,1)}, u32[]{:S(2)}) copy-start(bf16[1,704,2048]{2,1,0:T(8,128)(2,1)} %param.19) | copy-start | bytes 8650756
  11.2 10.3 %copy-start.11 = (f32[128,6]{0,1:T(8,128)S(1)}, f32[128,6]{0,1:T(8,128)}, u32[]{:S(2)}) copy-start(f32[128,6]{0,1:T(8,128)} %param.13) | copy-start | bytes 9220
  11.7 28.5 %copy-start.8 = (bf16[128,1024]{1,0:T(8,128)(2,1)S(1)}, bf16[128,1024]{1,0:T(8,128)(2,1)}, u32[]{:S(2)}) copy-start(bf16[128,1024]{1,0:T(8,128)(2,1)} %param.11) | copy-start | bytes 786436
  14.0 26.2 %all-to-all-start = ((bf16[16,24,1024]{2,1,0:T(8,128)(2,1)}), bf16[16,24,1024]{2,1,0:T(8,128)(2,1)}, u32[]{:S(2)}, u32[]{:S(2)}) async-start(bf16[16,24,1024]{2,1,0:T(8,128)(2,1)} %bitcast.74), calls=%async_computation | async-start | bytes 1572864 | tf_op jit(solution)/shard_map/all_to_all | solution.py:53
  21.4 46.9 %all-gather.3.cloned.1.call-start = ((), (), s32[]{:S(2)}) async-start(), calls=%async_computation.6 | async-start | bytes 2359296 | tf_op jit(solution)/shard_map/all_gather | solution.py:57
  21.9 44.1 %copy-start.9 = (f32[384]{0:T(512)}, f32[384]{0:T(512)S(1)}, u32[]{:S(2)}) copy-start(f32[384]{0:T(512)S(1)} %select_reduce_fusion) | copy-start | bytes 4612
  40.2 56.9 %all-gather.5.cloned.1.call-start = ((), (), s32[]{:S(2)}) async-start(), calls=%async_computation.8 | async-start | bytes 2359296 | tf_op jit(solution)/shard_map/all_gather | solution.py:58
  68.3 5.1 %copy-start.13 = (bf16[1,704,2048]{2,1,0:T(8,128)(2,1)S(1)}, bf16[1,704,2048]{2,1,0:T(8,128)(2,1)}, u32[]{:S(2)}) copy-start(bf16[1,704,2048]{2,1,0:T(8,128)(2,1)} %param.17) | copy-start | bytes 8650756
  68.3 5.1 %copy-start.15 = (bf16[384,2048]{1,0:T(8,128)(2,1)S(1)}, bf16[384,2048]{1,0:T(8,128)(2,1)}, u32[]{:S(2)}) copy-start(bf16[384,2048]{1,0:T(8,128)(2,1)} %all-gather.3.cloned.1.call-done) | copy-start | bytes 4718596
  97.0 4.1 %copy-start.12 = (bf16[1,704,2048]{2,1,0:T(8,128)(2,1)S(1)}, bf16[1,704,2048]{2,1,0:T(8,128)(2,1)}, u32[]{:S(2)}) copy-start(bf16[1,704,2048]{2,1,0:T(8,128)(2,1)} %param.18) | copy-start | bytes 8650756
  97.0 4.2 %copy-start.14 = (bf16[1,704,2048]{2,1,0:T(8,128)(2,1)S(1)}, bf16[1,704,2048]{2,1,0:T(8,128)(2,1)}, u32[]{:S(2)}) copy-start(bf16[1,704,2048]{2,1,0:T(8,128)(2,1)} %param.17) | copy-start | bytes 8650756
  104.9 5.8 %copy-start.7 = (bf16[128,1024]{1,0:T(8,128)(2,1)S(1)}, bf16[128,1024]{1,0:T(8,128)(2,1)}, u32[]{:S(2)}) copy-start(bf16[128,1024]{1,0:T(8,128)(2,1)} %param.10) | copy-start | bytes 786436
  104.9 37.7 %all-to-all-start.3 = ((bf16[16,24,2048]{2,1,0:T(8,128)(2,1)}), bf16[16,24,2048]{2,1,0:T(8,128)(2,1)}, u32[]{:S(2)}, u32[]{:S(2)}) async-start(bf16[16,24,2048]{2,1,0:T(8,128)(2,1)} %bitcast.78), calls=%async_computation.4 | async-start | bytes 3145728 | tf_op jit(solution)/shard_map/all_to_all | solution.py:109
  120.0 0.8 copy-start.4
  120.8 2.9 %copy-start.16 = (f32[384,704]{0,1:T(8,128)S(1)}, f32[384,704]{0,1:T(8,128)}, u32[]{:S(2)}) copy-start(f32[384,704]{0,1:T(8,128)} %fusion.7) | copy-start | bytes 3244036
  120.8 2.9 %copy-start.17 = (f32[384,704]{0,1:T(8,128)S(1)}, f32[384,704]{0,1:T(8,128)}, u32[]{:S(2)}) copy-start(f32[384,704]{0,1:T(8,128)} %fusion.9) | copy-start | bytes 3244036
  142.6 41.1 %all-to-all-start.1 = ((bf16[16,24,2048]{2,1,0:T(8,128)(2,1)}), bf16[16,24,2048]{2,1,0:T(8,128)(2,1)}, u32[]{:S(2)}, u32[]{:S(2)}) async-start(bf16[16,24,2048]{2,1,0:T(8,128)(2,1)} %bitcast.77), calls=%async_computation.1 | async-start | bytes 3145728 | tf_op jit(solution)/shard_map/all_to_all | solution.py:108
  151.8 39.4 %reduce-scatter.5.cloned.1.call-start = ((), (), s32[]{:S(2)}) async-start(), calls=%async_computation.9 | async-start | bytes 1572864 | tf_op jit(solution)/shard_map/reduce_scatter | solution.py:127
  151.8 12.5 %copy-start.3 = (bf16[704,2048]{1,0:T(8,128)(2,1)S(1)}, bf16[704,2048]{1,0:T(8,128)(2,1)}, u32[]{:S(2)}) copy-start(bf16[704,2048]{1,0:T(8,128)(2,1)} %param.16) | copy-start | bytes 8650756
  154.9 10.4 %copy-start.5 = (f32[128,704]{0,1:T(8,128)}, f32[128,704]{0,1:T(8,128)S(1)}, u32[]{:S(2)}) copy-start(f32[128,704]{0,1:T(8,128)S(1)} %fusion.45) | copy-start | bytes 1081348
  164.3 1.8 copy-start.2
  166.2 2.8 %copy-start.1 = (bf16[704,2048]{1,0:T(8,128)(2,1)S(1)}, bf16[704,2048]{1,0:T(8,128)(2,1)}, u32[]{:S(2)}) copy-start(bf16[704,2048]{1,0:T(8,128)(2,1)} %param.15) | copy-start | bytes 8650756
  168.9 14.8 %copy-start.10 = (f32[384]{0:T(512)S(1)}, f32[384]{0:T(512)}, u32[]{:S(2)}) copy-start(f32[384]{0:T(512)} %copy-done.9) | copy-start | bytes 4612
  170.6 43.3 %reduce-scatter.3.cloned.1.call-start = ((), (), s32[]{:S(2)}) async-start(), calls=%async_computation.7 | async-start | bytes 1572864 | tf_op jit(solution)/shard_map/reduce_scatter | solution.py:126
  183.7 2.6 %copy-start.6 = (f32[128,704]{0,1:T(8,128)S(1)}, f32[128,704]{0,1:T(8,128)}, u32[]{:S(2)}) copy-start(f32[128,704]{0,1:T(8,128)} %copy-done.5) | copy-start | bytes 1081348
Sparse Core Ops, SparseCore 0:
  40.3 27.9 all-gather.2
  69.8 27.1 all-gather.4
  170.7 20.4 reduce-scatter.4
  193.3 20.5 reduce-scatter.2
where the time goes:
time: 223 us; the launch traced here: 222 us
  waiting for transfers between devices  93.2 us (42%)
  blocking collectives  44.1 us (20%)
  matrix products  38.1 us (17%)
  starting transfers between devices  22.5 us (10%)
  between operations  14 us (6%)
  other arithmetic  6.47 us (3%)
  local copies, waits for them, and re-layouts  3.77 us (2%)
    all_to_all x1, blocking collectives, on_device(): lax.all_to_all(g_slots, 'expert', split_axis=0, concat_axis=0, tiled=True)  25.4 us
    all_gather x1, waiting for transfers between devices, on_device(): lax.all_gather(g_part, 'tensor', axis=1, tiled=True)  21 us
    reduce_scatter x1, waiting for transfers between devices, on_device(): lax.psum_scatter(early_value, 'tensor', scatter_dimension=1, tiled=True)  20.9 us
    all_to_all x1, waiting for transfers between devices, on_device(): lax.all_to_all(x_slots, 'expert', split_axis=0, concat_axis=0, tiled=True)  18.2 us
    all_to_all x1, waiting for transfers between devices, on_device(): lax.all_to_all(input_part, 'expert', split_axis=0, concat_axis=0, tiled=T...  16.3 us
    all_to_all x1, waiting for transfers between devices, on_device(): lax.all_to_all(value_part, 'expert', split_axis=0, concat_axis=0, tiled=T...  13.1 us
    all_gather x1, blocking collectives, on_device(): lax.all_gather(cotangent, 'tensor', axis=1, tiled=True)  9.42 us
    all_gather x1, blocking collectives, on_device(): lax.all_gather(tokens, 'tensor', axis=1, tiled=True)  9.24 us
  transfers between devices with their start and end apart: 7, of which 7 were waited for; matrix products, arithmetic and copies ran while one was open for 14% of the time, Pallas kernels for 0%

commit v1 on v0

--- a/solution.py
+++ b/solution.py
@@ -2,6 +2,11 @@
 import jax.numpy as jnp
 from jax import lax
 from jax.sharding import PartitionSpec as P
+
+
+def gather_over(x, axis, d):
+    stack = jnp.stack([x] * lax.axis_size(axis))
+    return jnp.concatenate(lax.all_to_all(stack, axis, 0, 0), axis=d)
 
 
 def silu_parts(pre_act):
@@ -55,7 +60,7 @@
     )
     x_recv, g_recv = (
         lax.all_gather(x_part, "tensor", axis=1, tiled=True),
-        lax.all_gather(g_part, "tensor", axis=1, tiled=True),
+        gather_over(g_part, "tensor", 1),
     )
 
     def owner_layout(values):

time: 223 us -> 226 us (1.013)
  waiting for transfers between devices: 93.2 us -> 86.9 us
  starting transfers between devices: 22.5 us -> 27.9 us
  local copies, waits for them, and re-layouts: 3.77 us -> 7.12 us
  matrix products: 38.1 us -> 34.9 us
    all_gather x1 -> x0, waiting for transfers between devices: 21 us -> none  [on_device(): lax.all_gather(g_part, 'tensor', axis=1, tiled=True)]
    all_to_all x0 -> x1, waiting for transfers between devices: none -> 18 us  [on_device(): lax.all_to_all(g_slots, 'expert', split_axis=0, concat_axis=0, tiled=True)]
    all_to_all x0 -> x1, starting transfers between devices: none -> 5.42 us  [on_device(): lax.all_to_all(g_slots, 'expert', split_axis=0, concat_axis=0, tiled=True)]
    reshape x0 -> x1, local copies, waits for them, and re-layouts: none -> 2.59 us  [gather_over(): return jnp.concatenate(lax.all_to_all(stack, axis, 0, 0), axis=d)]
  transfers between devices with their start and end apart: 7 -> 7, of which waited for: 7 -> 6; matrix products, arithmetic and copies ran while one was open for 14% -> 12% of each run, Pallas kernels for 0% -> 0%
where the time goes in v1:
time: 226 us; the launch traced here: 225 us
  waiting for transfers between devices  86.9 us (38%)
  blocking collectives  46 us (20%)
  matrix products  34.9 us (15%)
  starting transfers between devices  27.9 us (12%)
  between operations  14.1 us (6%)
  other arithmetic  7.98 us (4%)
  local copies, waits for them, and re-layouts  7.12 us (3%)
    all_to_all x1, blocking collectives, gather_over(): return jnp.concatenate(lax.all_to_all(stack, axis, 0, 0), axis=d)  27.3 us
    reduce_scatter x1, waiting for transfers between devices, on_device(): lax.psum_scatter(early_value, 'tensor', scatter_dimension=1, tiled=True)  20.9 us
    all_to_all x1, waiting for transfers between devices, on_device(): lax.all_to_all(g_slots, 'expert', split_axis=0, concat_axis=0, tiled=True)  18 us
    all_to_all x1, waiting for transfers between devices, on_device(): lax.all_to_all(x_slots, 'expert', split_axis=0, concat_axis=0, tiled=True)  16.4 us
    all_to_all x1, waiting for transfers between devices, on_device(): lax.all_to_all(input_part, 'expert', split_axis=0, concat_axis=0, tiled=T...  16.3 us
    all_to_all x1, waiting for transfers between devices, on_device(): lax.all_to_all(value_part, 'expert', split_axis=0, concat_axis=0, tiled=T...  13.1 us
    all_gather x1, blocking collectives, on_device(): lax.all_gather(cotangent, 'tensor', axis=1, tiled=True)  9.41 us
    all_gather x1, blocking collectives, on_device(): lax.all_gather(tokens, 'tensor', axis=1, tiled=True)  9.24 us
  transfers between devices with their start and end apart: 7, of which 6 were waited for; matrix products, arithmetic and copies ran while one was open for 12% of the time, Pallas kernels for 0%

profile of v1, /device:TPU:0, one launch (start us, length us, event | category | flops | bytes accessed | tf_op | source)
XLA Modules:
  0.0 224.8 jit_solution(6612554958952874614)
XLA Ops:
  7.2 0.0 copy-start
  7.2 0.9 copy.27
  8.1 0.1 eq.50
  8.3 0.1 eq.46
  8.4 0.7 broadcast_multiply_fusion
  9.1 1.7 reduce-window.6
  10.8 0.3 slice_reduce_fusion
  11.1 0.1 fusion.35
  11.2 0.0 copy-start.12
  11.2 0.1 reduce_sum.21
  11.4 0.1 copy.31
  11.5 0.1 copy.32
  11.5 0.2 fusion.16
  11.7 2.2 convolution_convert_fusion
  13.9 7.4 %all-to-all-start = ((bf16[16,24,1024]{2,1,0:T(8,128)(2,1)}), bf16[16,24,1024]{2,1,0:T(8,128)(2,1)}, u32[]{:S(2)}, u32[]{:S(2)}) async-start(bf16[16,24,1024]{2,1,0:T(8,128)(2,1)} %bitcast.78), calls=%async_computation | async-start | bytes 1572864 | tf_op jit(solution)/shard_map/all_to_all | solution.py:58
  21.4 0.1 copy.33
  21.5 0.1 broadcast_in_dim.27
  21.6 0.2 select_reduce_fusion
  21.9 0.6 copy-done.10
  22.4 0.0 copy-done.9
  22.4 1.2 multiply_convert_fusion
  23.7 16.4 %all-to-all-done = bf16[16,24,1024]{2,1,0:T(8,128)(2,1)} async-done(((bf16[16,24,1024]{2,1,0:T(8,128)(2,1)}), bf16[16,24,1024]{2,1,0:T(8,128)(2,1)}, u32[]{:S(2)}, u32[]{:S(2)}) %all-to-all-start) | async-done | bytes 786464 | tf_op jit(solution)/shard_map/all_to_all | solution.py:58
  40.1 5.4 %all-to-all-start.2 = ((bf16[16,24,1024]{2,1,0:T(8,128)(2,1)}), bf16[16,24,1024]{2,1,0:T(8,128)(2,1)}, u32[]{:S(2)}, u32[]{:S(2)}) async-start(bf16[16,24,1024]{2,1,0:T(8,128)(2,1)} %bitcast.77), calls=%async_computation.3 | async-start | bytes 1572864 | tf_op jit(solution)/shard_map/all_to_all | solution.py:59
  45.5 0.0 all-gather.2.cloned.1.call-start
  45.6 0.7 all-gather.2.cloned.1.call-update
  46.3 18.0 %all-to-all-done.2 = bf16[16,24,1024]{2,1,0:T(8,128)(2,1)} async-done(((bf16[16,24,1024]{2,1,0:T(8,128)(2,1)}), bf16[16,24,1024]{2,1,0:T(8,128)(2,1)}, u32[]{:S(2)}, u32[]{:S(2)}) %all-to-all-start.2) | async-done | bytes 786464 | tf_op jit(solution)/shard_map/all_to_all | solution.py:59
  64.3 1.5 pad_maximum_fusion
  65.8 27.3 %all_to_all.50 = bf16[2,384,1024]{2,1,0:T(8,128)(2,1)} all-to-all(bf16[2,384,1024]{2,1,0:T(8,128)(2,1)S(1)} %pad_maximum_fusion), channel_id=1, replica_groups=mesh['expert'=16,'tensor'=2] {'tensor'}, dimensions={0} | all-to-all | bytes 3145728 | tf_op jit(solution)/shard_map/all_to_all | solution.py:9
  93.1 2.6 %copy.34 = bf16[384,2,1024]{0,2,1:T(8,128)(2,1)} copy(bf16[384,2,1024]{2,0,1:T(8,128)(2,1)} %bitcast.76) | data formatting | bytes 3145728 | tf_op jit(solution)/shard_map/reshape | solution.py:9
  95.7 4.1 %fusion.7 = f32[384,704]{0,1:T(8,128)S(1)} fusion(bf16[384,2048]{1,0:T(8,128)(2,1)} %all-gather.2.cloned.1.call-done, bf16[1,704,2048]{2,1,0:T(8,128)(2,1)} %param.18), kind=kOutput, calls=%fused_computation.8 | convolution fusion | flops 1107296256 | bytes 5537792 | tf_op jit(solution)/shard_map/erd,efd->erf/dot_general | solution.py:79
  99.8 0.0 copy-done.14
  99.8 0.0 copy-done.15
  99.9 1.7 fusion.9
  101.6 0.1 copy-done.7
  101.7 1.9 fusion.21
  103.6 0.1 copy-done.13
  103.8 3.8 %fusion.14 = bf16[384,2048]{1,0:T(8,128)(2,1)} fusion(bf16[1,704,2048]{2,1,0:T(8,128)(2,1)S(1)} %copy-done.13, bf16[1,704,2048]{2,1,0:T(8,128)(2,1)S(1)} %copy-done.14, bf16[1,384,704]{1,2,0:T(8,128)(2,1)S(1)} %get-tuple-element.3, bf16[1,384,704]{1,2,0:T(8,128)(2,1)S(1)} %get-tuple-element.2), kind=kOutput, calls=%fused_computation.13 | convolution fusion | flops 2229075968 | bytes 8421376 | tf_op jit(solution)/shard_map/erf,efd->erd/dot_general | solution.py:92
  107.5 5.8 %all-to-all-start.4 = ((bf16[16,24,2048]{2,1,0:T(8,128)(2,1)}), bf16[16,24,2048]{2,1,0:T(8,128)(2,1)}, u32[]{:S(2)}, u32[]{:S(2)}) async-start(bf16[16,24,2048]{2,1,0:T(8,128)(2,1)} %bitcast.80), calls=%async_computation.5 | async-start | bytes 3145728 | tf_op jit(solution)/shard_map/all_to_all | solution.py:114
  113.3 9.2 %all_gather.9 = bf16[128,2048]{1,0:T(8,128)(2,1)S(1)} all-gather(bf16[128,1024]{1,0:T(8,128)(2,1)S(1)} %copy-done.8), channel_id=1, replica_groups=mesh['expert'=16,'tensor'=2] {'tensor'}, dimensions={1}, use_global_device_ids=true | all-gather | bytes 786432 | tf_op jit(solution)/shard_map/all_gather | solution.py:50
  122.6 0.8 copy-done.4
  123.4 2.9 %fusion.44 = f32[128,704]{0,1:T(8,128)S(1)} fusion(bf16[128,2048]{1,0:T(8,128)(2,1)S(1)} %all_gather.9, bf16[704,2048]{1,0:T(8,128)(2,1)} %param.14), kind=kOutput, calls=%fused_computation.63 | convolution fusion | flops 369098752 | bytes 3768320 | tf_op jit(solution)/shard_map/td,fd->tf/dot_general | solution.py:96
  126.3 2.7 %fusion.11 = bf16[384,2048]{1,0:T(8,128)(2,1)} fusion(bf16[1,704,2048]{2,1,0:T(8,128)(2,1)S(1)} %copy-done, f32[384,704]{0,1:T(8,128)S(1)} %copy-done.17, f32[384,704]{0,1:T(8,128)S(1)} %copy-done.19), kind=kOutput, calls=%fused_computation.12 | convolution fusion | flops 1109704704 | bytes 6619136 | tf_op jit(solution)/shard_map/erf,efd->erd/dot_general | solution.py:86
  128.9 16.3 %all-to-all-done.4 = bf16[16,24,2048]{2,1,0:T(8,128)(2,1)} async-done(((bf16[16,24,2048]{2,1,0:T(8,128)(2,1)}), bf16[16,24,2048]{2,1,0:T(8,128)(2,1)}, u32[]{:S(2)}, u32[]{:S(2)}) %all-to-all-start.4) | async-done | bytes 1572896 | tf_op jit(solution)/shard_map/all_to_all | solution.py:114
  145.2 9.2 %all-to-all-start.1 = ((bf16[16,24,2048]{2,1,0:T(8,128)(2,1)}), bf16[16,24,2048]{2,1,0:T(8,128)(2,1)}, u32[]{:S(2)}, u32[]{:S(2)}) async-start(bf16[16,24,2048]{2,1,0:T(8,128)(2,1)} %bitcast.79), calls=%async_computation.1 | async-start | bytes 3145728 | tf_op jit(solution)/shard_map/all_to_all | solution.py:113
  154.4 0.0 reduce-scatter.5.cloned.1.call-start
  154.4 0.0 copy-start.3
  154.4 3.0 %fusion.45 = f32[128,704]{0,1:T(8,128)S(1)} fusion(bf16[128,2048]{1,0:T(8,128)(2,1)} %copy-done.4, bf16[704,2048]{1,0:T(8,128)(2,1)} %param.15), kind=kOutput, calls=%fused_computation.64 | convolution fusion | flops 369098752 | bytes 3768320 | tf_op jit(solution)/shard_map/td,fd->tf/dot_general | solution.py:99
  157.5 9.4 %all_gather.11 = bf16[128,2048]{1,0:T(8,128)(2,1)S(1)} all-gather(bf16[128,1024]{1,0:T(8,128)(2,1)S(1)} %copy-done.9), channel_id=1, replica_groups=mesh['expert'=16,'tensor'=2] {'tensor'}, dimensions={1}, use_global_device_ids=true | all-gather | bytes 786432 | tf_op jit(solution)/shard_map/all_gather | solution.py:51
  166.9 0.9 fusion.46
  167.9 0.9 copy-done.2
  168.7 0.7 fusion.27
  169.4 2.1 fusion.47
  171.5 0.0 copy-start.11
  171.5 1.6 fusion.15
  173.2 0.0 reduce-scatter.5.cloned.1.call-update
  173.2 0.0 reduce-scatter.3.cloned.1.call-start
  173.2 13.1 %all-to-all-done.1 = bf16[16,24,2048]{2,1,0:T(8,128)(2,1)} async-done(((bf16[16,24,2048]{2,1,0:T(8,128)(2,1)}), bf16[16,24,2048]{2,1,0:T(8,128)(2,1)}, u32[]{:S(2)}, u32[]{:S(2)}) %all-to-all-start.1) | async-done | bytes 1572896 | tf_op jit(solution)/shard_map/all_to_all | solution.py:113
  186.3 2.6 %fusion.23 = f32[128,2048]{1,0:T(8,128)S(1)} fusion(bf16[384,2048]{1,0:T(8,128)(2,1)} %bitcast.7, f32[384]{0:T(512)S(1)} %copy-done.11, pred[384,128]{1,0:T(8,128)(4,1)S(1)} %fusion.16), kind=kOutput, calls=%fused_computation.39 | convolution fusion | flops 1208107008 | bytes 2672128 | tf_op jit(solution)/shard_map/st,sd->td/dot_general | solution.py:116
  188.9 3.5 %convolution_add_fusion.1 = f32[128,2048]{1,0:T(8,128)} fusion(f32[128,2048]{1,0:T(8,128)S(1)} %fusion.23, bf16[704,2048]{1,0:T(8,128)(2,1)} %param.16, f32[128,704]{0,1:T(8,128)S(1)} %copy-done.6, f32[128,704]{0,1:T(8,128)S(1)} %fusion.44), kind=kOutput, calls=%fused_computation.15 | convolution fusion | flops 369901568 | bytes 5701632 | tf_op jit(solution)/shard_map/dot_general | solution.py:102
  192.3 0.0 reduce-scatter.3.cloned.1.call-update
  192.4 1.5 reduce-scatter.5.cloned.1.call-done
  193.8 1.8 convert_element_type.76
  195.6 20.9 %reduce-scatter.3.cloned.1.call-done = f32[128,1024]{1,0:T(8,128)} async-done(((f32[128,2048]{1,0:T(8,128)}), f32[128,1024]{1,0:T(8,128)}) %reduce-scatter.3.cloned.1.call-update) | async-done | bytes 524304 | tf_op jit(solution)/shard_map/reduce_scatter | solution.py:131
  216.5 1.8 convert_element_type.67
  (33 shorter events, 0.1 us)
Async XLA Ops:
  7.2 94.4 %copy-start = (bf16[1,704,2048]{2,1,0:T(8,128)(2,1)S(1)}, bf16[1,704,2048]{2,1,0:T(8,128)(2,1)}, u32[]{:S(2)}) copy-start(bf16[1,704,2048]{2,1,0:T(8,128)(2,1)} %param.19) | copy-start | bytes 8650756
  11.2 10.2 %copy-start.12 = (f32[128,6]{0,1:T(8,128)S(1)}, f32[128,6]{0,1:T(8,128)}, u32[]{:S(2)}) copy-start(f32[128,6]{0,1:T(8,128)} %param.13) | copy-start | bytes 9220
  11.5 11.0 %copy-start.9 = (bf16[128,1024]{1,0:T(8,128)(2,1)S(1)}, bf16[128,1024]{1,0:T(8,128)(2,1)}, u32[]{:S(2)}) copy-start(bf16[128,1024]{1,0:T(8,128)(2,1)} %param.11) | copy-start | bytes 786436
  13.9 26.2 %all-to-all-start = ((bf16[16,24,1024]{2,1,0:T(8,128)(2,1)}), bf16[16,24,1024]{2,1,0:T(8,128)(2,1)}, u32[]{:S(2)}, u32[]{:S(2)}) async-start(bf16[16,24,1024]{2,1,0:T(8,128)(2,1)} %bitcast.78), calls=%async_computation | async-start | bytes 1572864 | tf_op jit(solution)/shard_map/all_to_all | solution.py:58
  21.9 0.6 copy-start.10
  40.1 24.2 %all-to-all-start.2 = ((bf16[16,24,1024]{2,1,0:T(8,128)(2,1)}), bf16[16,24,1024]{2,1,0:T(8,128)(2,1)}, u32[]{:S(2)}, u32[]{:S(2)}) async-start(bf16[16,24,1024]{2,1,0:T(8,128)(2,1)} %bitcast.77), calls=%async_computation.3 | async-start | bytes 1572864 | tf_op jit(solution)/shard_map/all_to_all | solution.py:59
  45.5 50.2 %all-gather.2.cloned.1.call-start = ((), (), s32[]{:S(2)}) async-start(), calls=%async_computation.7 | async-start | bytes 2359296 | tf_op jit(solution)/shard_map/all_gather | solution.py:62
  95.7 4.1 %copy-start.14 = (bf16[1,704,2048]{2,1,0:T(8,128)(2,1)S(1)}, bf16[1,704,2048]{2,1,0:T(8,128)(2,1)}, u32[]{:S(2)}) copy-start(bf16[1,704,2048]{2,1,0:T(8,128)(2,1)} %param.17) | copy-start | bytes 8650756
  95.7 4.1 %copy-start.15 = (bf16[384,2048]{1,0:T(8,128)(2,1)S(1)}, bf16[384,2048]{1,0:T(8,128)(2,1)}, u32[]{:S(2)}) copy-start(bf16[384,2048]{1,0:T(8,128)(2,1)} %all-gather.2.cloned.1.call-done) | copy-start | bytes 4718596
  99.8 1.7 copy-start.16
  99.9 1.8 copy-start.7
  101.5 2.1 copy-start.18
  101.7 2.1 copy-start.13
  107.5 5.8 %copy-start.8 = (bf16[128,1024]{1,0:T(8,128)(2,1)S(1)}, bf16[128,1024]{1,0:T(8,128)(2,1)}, u32[]{:S(2)}) copy-start(bf16[128,1024]{1,0:T(8,128)(2,1)} %param.10) | copy-start | bytes 786436
  107.5 37.7 %all-to-all-start.4 = ((bf16[16,24,2048]{2,1,0:T(8,128)(2,1)}), bf16[16,24,2048]{2,1,0:T(8,128)(2,1)}, u32[]{:S(2)}, u32[]{:S(2)}) async-start(bf16[16,24,2048]{2,1,0:T(8,128)(2,1)} %bitcast.80), calls=%async_computation.5 | async-start | bytes 3145728 | tf_op jit(solution)/shard_map/all_to_all | solution.py:114
  122.6 0.8 copy-start.4
  123.4 2.9 %copy-start.17 = (f32[384,704]{0,1:T(8,128)S(1)}, f32[384,704]{0,1:T(8,128)}, u32[]{:S(2)}) copy-start(f32[384,704]{0,1:T(8,128)} %copy-done.16) | copy-start | bytes 3244036
  123.4 2.9 %copy-start.19 = (f32[384,704]{0,1:T(8,128)S(1)}, f32[384,704]{0,1:T(8,128)}, u32[]{:S(2)}) copy-start(f32[384,704]{0,1:T(8,128)} %copy-done.18) | copy-start | bytes 3244036
  145.2 41.1 %all-to-all-start.1 = ((bf16[16,24,2048]{2,1,0:T(8,128)(2,1)}), bf16[16,24,2048]{2,1,0:T(8,128)(2,1)}, u32[]{:S(2)}, u32[]{:S(2)}) async-start(bf16[16,24,2048]{2,1,0:T(8,128)(2,1)} %bitcast.79), calls=%async_computation.1 | async-start | bytes 3145728 | tf_op jit(solution)/shard_map/all_to_all | solution.py:113
  154.4 39.4 %reduce-scatter.5.cloned.1.call-start = ((), (), s32[]{:S(2)}) async-start(), calls=%async_computation.9 | async-start | bytes 1572864 | tf_op jit(solution)/shard_map/reduce_scatter | solution.py:132
  154.4 12.5 %copy-start.3 = (bf16[704,2048]{1,0:T(8,128)(2,1)S(1)}, bf16[704,2048]{1,0:T(8,128)(2,1)}, u32[]{:S(2)}) copy-start(bf16[704,2048]{1,0:T(8,128)(2,1)} %param.16) | copy-start | bytes 8650756
  157.5 10.4 %copy-start.5 = (f32[128,704]{0,1:T(8,128)}, f32[128,704]{0,1:T(8,128)S(1)}, u32[]{:S(2)}) copy-start(f32[128,704]{0,1:T(8,128)S(1)} %fusion.45) | copy-start | bytes 1081348
  166.9 1.8 copy-start.2
  168.7 2.8 %copy-start.1 = (bf16[704,2048]{1,0:T(8,128)(2,1)S(1)}, bf16[704,2048]{1,0:T(8,128)(2,1)}, u32[]{:S(2)}) copy-start(bf16[704,2048]{1,0:T(8,128)(2,1)} %param.15) | copy-start | bytes 8650756
  171.5 14.8 %copy-start.11 = (f32[384]{0:T(512)S(1)}, f32[384]{0:T(512)}, u32[]{:S(2)}) copy-start(f32[384]{0:T(512)} %copy-done.10) | copy-start | bytes 4612
  173.2 43.3 %reduce-scatter.3.cloned.1.call-start = ((), (), s32[]{:S(2)}) async-start(), calls=%async_computation.8 | async-start | bytes 1572864 | tf_op jit(solution)/shard_map/reduce_scatter | solution.py:131
  186.3 2.6 %copy-start.6 = (f32[128,704]{0,1:T(8,128)S(1)}, f32[128,704]{0,1:T(8,128)}, u32[]{:S(2)}) copy-start(f32[128,704]{0,1:T(8,128)} %copy-done.5) | copy-start | bytes 1081348
Sparse Core Ops, SparseCore 0:
  47.9 32.5 all-gather.1
  173.3 20.4 reduce-scatter.4
  196.1 20.3 reduce-scatter.2
